TPU v7x, 512 devices: a whole 4x4x16 slice. The times are simulated.
512 devices in a mesh: seq: 64 (over z, y), ch: 8 (over x, core).
Axes of the slice: x: 4, y: 4, z: 16, core: 2. Of those that a mesh axis runs over, the one named last changes fastest.
Arguments:
- normalized_layer_entry: bfloat16 [8192, 4096], P('seq', 'ch'), may hold values from -6 to 6
- short_outer_query: bfloat16 [8192, 4096], P('seq', 'ch'), may hold values from -6 to 6
- short_inner_key: bfloat16 [8192, 4096], P('seq', 'ch'), may hold values from -6 to 6
- short_frozen_value: bfloat16 [8192, 4096], P('seq', 'ch'), may hold values from -6 to 6
- medium_outer_query: bfloat16 [8192, 4096], P('seq', 'ch'), may hold values from -6 to 6
- medium_inner_key: bfloat16 [8192, 4096], P('seq', 'ch'), may hold values from -6 to 6
- cotangent: bfloat16 [8192, 4096], P('seq', 'ch'), may hold values from -6 to 6
- adapter_down_factor: bfloat16 [64, 32, 4096], P('seq', None, 'ch'), may hold values from -0.09375 to 0.09375
- adapter_up_factor: bfloat16 [64, 32, 4096], P('seq', None, 'ch'), may hold values from -1 to 1
- token_clade: int32 [8192, 1], P('seq'), may hold values from 0 to 63; in each aligned block of 128 rows (0 to 127, 128 to 255, ...) at most 4 rows name the same one
- clade_storage_slot: int32 [64], replicated, may hold values from 0 to 63, each once
- short_group_filter: float32 [256, 7], P('ch'), may hold values from -2.4 to 2.4
- medium_undamped_filter: float32 [256, 128], P('ch'), may hold values from -0.6 to 0.6
- medium_decay_rate: float32 [256], P('ch'), may hold values from 0.003 to 0.06
Outputs:
- midrange_response: bfloat16 [8192, 4096], P('seq', 'ch')
- layer_entry_derivative: bfloat16 [8192, 4096], P('seq', 'ch')
- lowdim_projector_derivative: float32 [64, 32, 4096], P('seq', None, 'ch')
- lowdim_expander_derivative: float32 [64, 32, 4096], P('seq', None, 'ch')
- brief_convolution_derivative: float32 [256, 7], P('ch')
- midrange_raw_response_derivative: float32 [256, 128], P('ch')
Inputs may be any that keep to these rules, and one draw needn't show every extreme that they name: `token_clade`: among the 128 tokens of one device, no clade is named more than 4 times, a bound that some block reaches. `clade_storage_slot`: each slot holds exactly one clade's adapter.
All inputs are finite; a program needn't handle non-finite values.
Results may differ from a plain program's by a relative error of at most 0.012.
Values may be sent and summed in bfloat16 or wider, within the bound.
A program may use at most 64 MiB of HBM per device.

v0:
```python
import math
import jax
import jax.numpy as jnp
from jax import lax
from jax.sharding import PartitionSpec as P


def passed_along(value, axis, steps):
    count = lax.axis_size(axis)
    first, last = (max(0, -steps), min(count, count - steps))
    return lax.ppermute(value, axis, [(source, source + steps) for source in range(first, last)])


def band_matrix(kernel, out_len):
    groups, taps = kernel.shape
    full_len = out_len + taps - 1
    reversed_taps = kernel[:, ::-1]
    padded = jnp.concatenate(
        [reversed_taps, jnp.zeros((groups, full_len + 1 - taps), kernel.dtype)], axis=1
    )
    repeated_groups = jnp.tile(padded, (1, out_len))[:, : out_len * full_len]
    return repeated_groups.reshape(groups, out_len, full_len)


def causal_local(extended, kernel):
    groups, taps = kernel.shape
    full_len, feature_lanes = extended.shape
    out_len = full_len - taps + 1
    group_size = feature_lanes // groups
    per_block = math.gcd(groups, 8)
    blocks = groups // per_block
    shaped = extended.reshape(full_len, blocks, per_block, group_size).transpose(1, 2, 3, 0)
    kernel_blocks = kernel.reshape(blocks, per_block, taps)

    def one_block(pair):
        data, kern = pair
        band = band_matrix(kern, out_len)
        return jnp.einsum("gts,gcs->gct", band, data, precision=lax.Precision.HIGHEST)

    result = lax.map(one_block, (shaped, kernel_blocks))
    return result.transpose(3, 0, 1, 2).reshape(out_len, feature_lanes)


def to_slots(placing, values):
    return jnp.dot(placing, values, preferred_element_type=jnp.float32).astype(jnp.bfloat16)


def contract_last(left, right):
    return lax.dot_general(
        left, right, (((1,), (1,)), ((), ())), preferred_element_type=jnp.float32
    )


def contract_first(left, right):
    return lax.dot_general(
        left, right, (((0,), (0,)), ((), ())), preferred_element_type=jnp.float32
    )


def select_codes(products, owner_hot):
    sequence_length = products.shape[0]
    return jnp.sum(
        products.reshape(sequence_length, owner_hot.shape[1], -1) * owner_hot[:, :, None], axis=1
    )


def spread_codes(lineage_labels, owner_hot):
    sequence_length = lineage_labels.shape[0]
    return (
        (owner_hot[:, :, None] * lineage_labels.astype(jnp.float32)[:, None, :])
        .reshape(sequence_length, -1)
        .astype(jnp.bfloat16)
    )


def on_device(
    normalized_layer_entry,
    short_outer_query,
    short_inner_key,
    short_frozen_value,
    medium_outer_query,
    medium_inner_key,
    cotangent,
    adapter_down_factor,
    adapter_up_factor,
    token_clade,
    clade_storage_slot,
    short_group_filter,
    medium_undamped_filter,
    medium_decay_rate,
):
    sequence_length, feature_lanes = normalized_layer_entry.shape
    seq_count = lax.axis_size("seq")
    capacity = max(2, 2 * sequence_length // seq_count)
    slot_count = seq_count * capacity
    lowdim_breadth = adapter_down_factor.shape[1]
    short_len = short_group_filter.shape[1]
    medium_len = medium_undamped_filter.shape[1]
    group_size = feature_lanes // short_group_filter.shape[0]
    clade_hot = (
        token_clade[:, 0][:, None] == jnp.arange(seq_count, dtype=jnp.int32)[None, :]
    ).astype(jnp.float32)
    owner_token = jnp.sum(clade_hot * clade_storage_slot[None, :].astype(jnp.float32), axis=1)
    earlier_mask = (
        jnp.arange(sequence_length)[:, None] > jnp.arange(sequence_length)[None, :]
    ).astype(jnp.float32)
    earlier = jnp.dot(earlier_mask, clade_hot, precision=lax.Precision.HIGHEST)
    rank_inside = jnp.sum(clade_hot * earlier, axis=1)
    position = owner_token * capacity + rank_inside
    placing = (jnp.arange(slot_count, dtype=jnp.float32)[:, None] == position[None, :]).astype(
        jnp.bfloat16
    )
    owner_hot = (owner_token[:, None] == jnp.arange(seq_count, dtype=jnp.float32)[None, :]).astype(
        jnp.float32
    )
    all_down, all_up = (
        lax.all_gather(adapter_down_factor, "seq", axis=0, tiled=True),
        lax.all_gather(adapter_up_factor, "seq", axis=0, tiled=True),
    )
    flat_down = all_down.reshape(seq_count * lowdim_breadth, feature_lanes)
    flat_up = all_up.reshape(seq_count * lowdim_breadth, feature_lanes)
    lineage_labels = lax.psum(
        select_codes(contract_last(normalized_layer_entry, flat_down), owner_hot), "ch"
    ).astype(jnp.bfloat16)
    adapter_update = (
        0.5
        * jnp.dot(
            spread_codes(lineage_labels, owner_hot), flat_up, preferred_element_type=jnp.float32
        )
    ).astype(jnp.bfloat16)
    short_in = (
        short_inner_key.astype(jnp.float32)
        * (short_frozen_value.astype(jnp.float32) + adapter_update.astype(jnp.float32))
    ).astype(jnp.bfloat16)
    short_head = passed_along(short_in[sequence_length - (short_len - 1) :], "seq", 1)
    short_ext = jnp.concatenate([short_head, short_in], axis=0).astype(jnp.float32)
    taps_index = jnp.arange(medium_len, dtype=jnp.float32)
    decay_envelope = jnp.exp(-medium_decay_rate[:, None] * taps_index[None, :])
    medium_taps = medium_undamped_filter * decay_envelope
    short_conv, short_pull = jax.vjp(lambda kern: causal_local(short_ext, kern), short_group_filter)
    medium_operator_input = (
        medium_inner_key.astype(jnp.float32) * short_outer_query.astype(jnp.float32) * short_conv
    ).astype(jnp.bfloat16)
    medium_head = passed_along(
        medium_operator_input[sequence_length - (medium_len - 1) :], "seq", 1
    )
    medium_ext = jnp.concatenate([medium_head, medium_operator_input], axis=0).astype(jnp.float32)
    medium_conv, medium_pull = jax.vjp(lambda kern: causal_local(medium_ext, kern), medium_taps)
    midrange_response = (medium_outer_query.astype(jnp.float32) * medium_conv).astype(jnp.bfloat16)
    medium_gradient = (
        cotangent.astype(jnp.float32) * medium_outer_query.astype(jnp.float32)
    ).astype(jnp.bfloat16)
    (medium_tap_grad,) = medium_pull(medium_gradient.astype(jnp.float32))
    medium_next = passed_along(medium_gradient[: medium_len - 1], "seq", -1)
    medium_span = jnp.concatenate([medium_gradient, medium_next], axis=0).astype(jnp.float32)
    medium_in_grad = causal_local(medium_span[::-1], medium_taps)[::-1]
    short_grad = (
        medium_in_grad
        * medium_inner_key.astype(jnp.float32)
        * short_outer_query.astype(jnp.float32)
    ).astype(jnp.bfloat16)
    (short_tap_grad,) = short_pull(short_grad.astype(jnp.float32))
    short_next = passed_along(short_grad[: short_len - 1], "seq", -1)
    short_span = jnp.concatenate([short_grad, short_next], axis=0).astype(jnp.float32)
    short_in_grad = causal_local(short_span[::-1], short_group_filter)[::-1]
    short_total, medium_total = lax.psum((short_tap_grad, medium_tap_grad * decay_envelope), "seq")
    filter_gradient_scale = 1.0 / math.sqrt(sequence_length * seq_count * group_size)
    brief_convolution_derivative = short_total * filter_gradient_scale
    midrange_raw_response_derivative = medium_total * filter_gradient_scale
    correction_delta_derivative = (
        0.5 * short_in_grad * short_inner_key.astype(jnp.float32)
    ).astype(jnp.bfloat16)
    correction_multiplier = 1.0 / math.sqrt(sequence_length)
    lineage_labels_derivative = lax.psum(
        select_codes(contract_last(correction_delta_derivative, flat_up), owner_hot), "ch"
    ).astype(jnp.bfloat16)
    layer_entry_derivative = jnp.dot(
        spread_codes(lineage_labels_derivative, owner_hot),
        flat_down,
        preferred_element_type=jnp.float32,
    ).astype(jnp.bfloat16)
    packed = (
        to_slots(placing, normalized_layer_entry).reshape(seq_count, capacity, feature_lanes),
        to_slots(placing, lineage_labels).reshape(seq_count, capacity, lowdim_breadth),
        to_slots(placing, correction_delta_derivative).reshape(seq_count, capacity, feature_lanes),
        to_slots(placing, lineage_labels_derivative).reshape(seq_count, capacity, lowdim_breadth),
    )
    got_input, got_codes, got_delta, got_codes_grad = (
        lax.all_to_all(packed[0], "seq", split_axis=0, concat_axis=0, tiled=True),
        lax.all_to_all(packed[1], "seq", split_axis=0, concat_axis=0, tiled=True),
        lax.all_to_all(packed[2], "seq", split_axis=0, concat_axis=0, tiled=True),
        lax.all_to_all(packed[3], "seq", split_axis=0, concat_axis=0, tiled=True),
    )
    lowdim_expander_derivative = (
        contract_first(
            got_codes.reshape(slot_count, lowdim_breadth),
            got_delta.reshape(slot_count, feature_lanes),
        )
        * correction_multiplier
    )
    lowdim_projector_derivative = (
        contract_first(
            got_codes_grad.reshape(slot_count, lowdim_breadth),
            got_input.reshape(slot_count, feature_lanes),
        )
        * correction_multiplier
    )
    return (
        midrange_response,
        layer_entry_derivative,
        lowdim_projector_derivative.reshape(1, lowdim_breadth, feature_lanes),
        lowdim_expander_derivative.reshape(1, lowdim_breadth, feature_lanes),
        brief_convolution_derivative,
        midrange_raw_response_derivative,
    )


def solution(mesh):
    return jax.shard_map(
        on_device,
        mesh=mesh,
        in_specs=(
            P("seq", "ch"),
            P("seq", "ch"),
            P("seq", "ch"),
            P("seq", "ch"),
            P("seq", "ch"),
            P("seq", "ch"),
            P("seq", "ch"),
            P("seq", None, "ch"),
            P("seq", None, "ch"),
            P("seq", None),
            P(),
            P("ch", None),
            P("ch", None),
            P("ch"),
        ),
        out_specs=(
            P("seq", "ch"),
            P("seq", "ch"),
            P("seq", None, "ch"),
            P("seq", None, "ch"),
            P("ch", None),
            P("ch", None),
        ),
        check_vma=False,
    )
```

profile of v0, /device:TPU:2, one launch (start us, length us, event | category | flops | bytes accessed | tf_op | source)
XLA Modules:
  0.0 734.2 jit_solution(13968584702329256065)
XLA Ops:
  15.2 20.2 %all-to-all-start.1 = ((bf16[64,4,512]{2,1,0:T(4,128)(2,1)}), bf16[64,4,512]{2,1,0:T(4,128)(2,1)}, u32[]{:S(2)}, u32[]{:S(2)}) async-start(bf16[64,4,512]{2,1,0:T(4,128)(2,1)} %reshape.205), calls=%async_computation.1 | async-start | bytes 524288 | tf_op jit(solution)/shard_map/all_to_all | solution.py:189
  37.7 10.5 %while.70 = (s32[]{:T(128)}, f32[4,8,16,128]{3,2,1,0:T(8,128)S(1)}, f32[4,8,16,255]{3,2,1,0:T(8,128)S(1)}, f32[4,8,128]{2,1,0:T(8,128)S(1)}, s32[]{:T(128)}, /*index=5*/f32[]{:T(128)}) while((s32[]{:T(128)}, f32[4,8,16,128]{3,2,1,0:T(8,128)S(1)}, f32[4,8,16,255]{3,2,1,0:T(8,128)S(1)}, f32[4,8,128]{2,1,0:T(8,128)S(1)}, s32[]{:T(128)}, ...), condition=%wide.region_8.9_spmd, body=%wide.region_7.8_spmd.sunk | while | flops 50135040 | bytes 6509645 | solution.py:40
  51.8 3.2 collective-permute-done.3
  56.5 14.3 %while.71 = (s32[]{:T(128)}, f32[4,8,16,128]{3,2,1,0:T(8,128)}, f32[4,8,16,134]{3,2,1,0:T(8,128)S(1)}, f32[4,8,7]{2,1,0:T(8,128)S(1)}, s32[]{:T(128)}, /*index=5*/f32[]{:T(128)}) while((s32[]{:T(128)}, f32[4,8,16,128]{3,2,1,0:T(8,128)}, f32[4,8,16,134]{3,2,1,0:T(8,128)S(1)}, f32[4,8,7]{2,1,0:T(8,128)S(1)}, s32[]{:T(128)}, ...), condition=%wide.region_10.11_spmd, body=%wide.region_9.10_spmd.sunk | while | flops 26345472 | bytes 5110381 | solution.py:40
  74.1 83.2 %all-gather.5.cloned.1.call-done = bf16[64,32,512]{2,1,0:T(8,128)(2,1)} async-done(((bf16[1,32,512]{2,1,0:T(8,128)(2,1)}), bf16[64,32,512]{2,1,0:T(8,128)(2,1)}) %all-gather.5.cloned.1.call-update) | async-done | bytes 2097168 | tf_op jit(solution)/shard_map/all_gather | solution.py:118
  157.3 4.0 fusion.42
  161.3 135.9 %all-gather.3.cloned.1.call-done = bf16[64,32,512]{2,1,0:T(8,128)(2,1)} async-done(((bf16[1,32,512]{2,1,0:T(8,128)(2,1)}), bf16[64,32,512]{2,1,0:T(8,128)(2,1)}) %all-gather.3.cloned.1.call-update) | async-done | bytes 2097168 | tf_op jit(solution)/shard_map/all_gather | solution.py:117
  297.3 4.0 fusion.45
  301.3 20.7 %all-reduce.7 = (bf16[128,32]{0,1:T(8,128)(2,1)S(1)}, bf16[128,32]{0,1:T(8,128)(2,1)S(1)}) all-reduce(f32[128,32]{0,1:T(8,128)S(1)} %fusion.45, f32[128,32]{0,1:T(8,128)S(1)} %fusion.42), channel_id=1, replica_groups=mesh['seq'=64,'ch'=8] {'ch'}, use_global_device_ids=true, to_apply=%region_2.0 | all-reduce | flops 8192 | bytes 49152 | tf_op jit(solution)/shard_map/psum | solution.py:122
  322.0 4.2 fusion.72
  326.2 2.2 collective-permute-start
  328.7 3.1 fusion.69
  333.9 11.6 %all-to-all-start.3 = ((bf16[64,4,512]{2,1,0:T(4,128)(2,1)}), bf16[64,4,512]{2,1,0:T(4,128)(2,1)}, u32[]{:S(2)}, u32[]{:S(2)}) async-start(bf16[64,4,512]{2,1,0:T(4,128)(2,1)} %reshape.208), calls=%async_computation.3 | async-start | bytes 524288 | tf_op jit(solution)/shard_map/all_to_all | solution.py:191
  346.3 14.3 %while.68 = (s32[]{:T(128)}, f32[4,8,16,128]{3,2,1,0:T(8,128)}, f32[4,8,16,134]{3,2,1,0:T(8,128)S(1)}, f32[4,8,7]{2,1,0:T(8,128)S(1)}, s32[]{:T(128)}, /*index=5*/f32[]{:T(128)}) while((s32[]{:T(128)}, f32[4,8,16,128]{3,2,1,0:T(8,128)}, f32[4,8,16,134]{3,2,1,0:T(8,128)S(1)}, f32[4,8,7]{2,1,0:T(8,128)S(1)}, s32[]{:T(128)}, ...), condition=%wide.region_4.5_spmd, body=%wide.region_3.0_spmd.sunk | while | flops 26345472 | bytes 5110381 | solution.py:40
  364.1 4.0 collective-permute-start.1
  368.2 14.1 %all-to-all-start.2 = ((bf16[64,4,32]{2,1,0:T(4,128)(2,1)}), bf16[64,4,32]{2,1,0:T(4,128)(2,1)S(1)}, u32[]{:S(2)}, u32[]{:S(2)}) async-start(bf16[64,4,32]{2,1,0:T(4,128)(2,1)} %bitcast.49), calls=%async_computation.2 | async-start | bytes 131072 | tf_op jit(solution)/shard_map/all_to_all | solution.py:190
  382.8 14.1 %while.72 = (s32[]{:T(128)}, f32[4,8,7]{2,1,0:T(8,128)}, f32[4,8,16,128]{3,2,1,0:T(8,128)S(1)}, f32[4,8,16,134]{3,2,1,0:T(8,128)S(1)}, s32[]{:T(128)}, /*index=5*/s32[]{:T(128)}, f32[]{:T(128)}) while((s32[]{:T(128)}, f32[4,8,7]{2,1,0:T(8,128)}, f32[4,8,16,128]{3,2,1,0:T(8,128)S(1)}, f32[4,8,16,134]{3,2,1,0:T(8,128)S(1)}, s32[]{:T(128)}, ...), condition=%wide.region_16.17_spmd, body=%wide.region_14.16_spmd.sunk | while | flops 26482636 | bytes 4614565 | solution.py:40
  397.7 15.4 %all-to-all-start = ((bf16[64,4,32]{2,1,0:T(4,128)(2,1)}), bf16[64,4,32]{2,1,0:T(4,128)(2,1)S(1)}, u32[]{:S(2)}, u32[]{:S(2)}) async-start(bf16[64,4,32]{2,1,0:T(4,128)(2,1)} %bitcast.46), calls=%async_computation | async-start | bytes 131072 | tf_op jit(solution)/shard_map/all_to_all | solution.py:192
  413.1 1.8 fusion.78
  414.8 13.2 %all-to-all-done = bf16[64,4,32]{2,1,0:T(4,128)(2,1)S(1)} async-done(((bf16[64,4,32]{2,1,0:T(4,128)(2,1)}), bf16[64,4,32]{2,1,0:T(4,128)(2,1)S(1)}, u32[]{:S(2)}, u32[]{:S(2)}) %all-to-all-start) | async-done | bytes 16416 | tf_op jit(solution)/shard_map/all_to_all | solution.py:192
  428.0 1.8 fusion.76
  431.9 7.9 %while.73 = (s32[]{:T(128)}, f32[4,8,128]{2,1,0:T(8,128)S(1)}, f32[4,8,16,128]{3,2,1,0:T(8,128)S(1)}, f32[4,8,16,255]{3,2,1,0:T(8,128)S(1)}, s32[]{:T(128)}, /*index=5*/s32[]{:T(128)}, f32[]{:T(128)}) while((s32[]{:T(128)}, f32[4,8,128]{2,1,0:T(8,128)S(1)}, f32[4,8,16,128]{3,2,1,0:T(8,128)S(1)}, f32[4,8,16,255]{3,2,1,0:T(8,128)S(1)}, ...), condition=%wide.region_20.21_spmd, body=%wide.region_18.20_spmd.sunk | while | flops 50395136 | bytes 6505573 | solution.py:40
  439.8 275.1 %all-reduce.6 = (f32[32,7]{0,1:T(8,128)S(1)}, f32[32,128]{1,0:T(8,128)S(1)}) all-reduce(f32[32,7]{0,1:T(8,128)S(1)} %copy.96, f32[32,128]{1,0:T(8,128)S(1)} %bitcast_multiply_fusion), channel_id=1, replica_groups=mesh['seq'=64,'ch'=8] {'seq'}, use_global_device_ids=true, to_apply=%region_17.18 | all-reduce | flops 4320 | bytes 34560 | tf_op jit(solution)/shard_map/psum | solution.py:166
  716.1 10.5 %while.69 = (s32[]{:T(128)}, f32[4,8,16,128]{3,2,1,0:T(8,128)S(1)}, f32[4,8,16,255]{3,2,1,0:T(8,128)S(1)}, f32[4,8,128]{2,1,0:T(8,128)S(1)}, s32[]{:T(128)}, /*index=5*/f32[]{:T(128)}) while((s32[]{:T(128)}, f32[4,8,16,128]{3,2,1,0:T(8,128)S(1)}, f32[4,8,16,255]{3,2,1,0:T(8,128)S(1)}, f32[4,8,128]{2,1,0:T(8,128)S(1)}, s32[]{:T(128)}, ...), condition=%wide.region_6.7_spmd, body=%wide.region_5.6_spmd.sunk | while | flops 50135040 | bytes 6509645 | solution.py:40
  (275 shorter events, 101.2 us)
Async XLA Ops:
  7.2 7.0 copy-start
  7.2 28.9 %copy-start.12 = (f32[32]{0:T(128)S(1)}, f32[32]{0:T(128)}, u32[]{:S(2)}) copy-start(f32[32]{0:T(128)} %param.39) | copy-start | bytes 388
  7.2 29.0 %copy-start.3 = (f32[32,128]{1,0:T(8,128)S(1)}, f32[32,128]{1,0:T(8,128)}, u32[]{:S(2)}) copy-start(f32[32,128]{1,0:T(8,128)} %param.38) | copy-start | bytes 49156
  7.2 150.0 %all-gather.5.cloned.1.call-start = ((), (), s32[]{:S(2)}) async-start(), calls=%async_computation.5 | async-start | bytes 2129920 | tf_op jit(solution)/shard_map/all_gather | solution.py:118
  10.0 26.6 %collective-permute-start.2 = (bf16[127,512]{0,1:T(8,128)(2,1)S(1)}, bf16[127,512]{0,1:T(8,128)(2,1)S(1)}, u32[]{:S(2)}, u32[]{:S(2)}) collective-permute-start(bf16[127,512]{0,1:T(8,128)(2,1)S(1)} %bitcast.204), channel_id=1, source_target_pairs={{8,0},{16,8},{24,16},{32,24},{40,32},{48,40},{56,48},{64,56},{72,6... | collective-permute-start | bytes 390152 | tf_op jit(solution)/shard_map/ppermute | solution.py:11
  13.7 0.5 copy-start.9
  14.2 21.2 %copy-start.7 = (f32[128]{0:T(128)}, f32[128]{0:T(128)S(1)}, u32[]{:S(2)}) copy-start(f32[128]{0:T(128)S(1)} %multiply_add_fusion) | copy-start | bytes 1540
  15.2 318.7 %all-to-all-start.1 = ((bf16[64,4,512]{2,1,0:T(4,128)(2,1)}), bf16[64,4,512]{2,1,0:T(4,128)(2,1)}, u32[]{:S(2)}, u32[]{:S(2)}) async-start(bf16[64,4,512]{2,1,0:T(4,128)(2,1)} %reshape.205), calls=%async_computation.1 | async-start | bytes 524288 | tf_op jit(solution)/shard_map/all_to_all | solution.py:189
  35.4 261.9 %all-gather.3.cloned.1.call-start = ((), (), s32[]{:S(2)}) async-start(), calls=%async_computation.4 | async-start | bytes 2129920 | tf_op jit(solution)/shard_map/all_gather | solution.py:117
  36.1 0.5 copy-start.5
  37.7 10.8 %copy-start.1 = (bf16[128,512]{1,0:T(8,128)(2,1)S(1)}, bf16[128,512]{1,0:T(8,128)(2,1)}, u32[]{:S(2)}) copy-start(bf16[128,512]{1,0:T(8,128)(2,1)} %param.27) | copy-start | bytes 393220
  37.7 13.9 %copy-start.4 = (f32[32,7]{0,1:T(8,128)S(1)}, f32[32,7]{0,1:T(8,128)}, u32[]{:S(2)}) copy-start(f32[32,7]{0,1:T(8,128)} %param.37) | copy-start | bytes 2692
  49.4 5.5 collective-permute-start.3
  56.5 15.6 %copy-start.8 = (f32[128]{0:T(128)S(1)}, f32[128]{0:T(128)}, u32[]{:S(2)}) copy-start(f32[128]{0:T(128)} %copy-done.7) | copy-start | bytes 1540
  70.8 86.4 %copy-start.2 = (bf16[128,512]{1,0:T(8,128)(2,1)S(1)}, bf16[128,512]{1,0:T(8,128)(2,1)}, u32[]{:S(2)}) copy-start(bf16[128,512]{1,0:T(8,128)(2,1)} %param.28) | copy-start | bytes 393220
  161.3 160.7 %copy-start.11 = (bf16[128,512]{1,0:T(8,128)(2,1)S(1)}, bf16[128,512]{1,0:T(8,128)(2,1)}, u32[]{:S(2)}) copy-start(bf16[128,512]{1,0:T(8,128)(2,1)} %param.29) | copy-start | bytes 393220
  322.0 6.6 copy-start.10
  326.2 7.3 collective-permute-start
  333.9 34.3 %all-to-all-start.3 = ((bf16[64,4,512]{2,1,0:T(4,128)(2,1)}), bf16[64,4,512]{2,1,0:T(4,128)(2,1)}, u32[]{:S(2)}, u32[]{:S(2)}) async-start(bf16[64,4,512]{2,1,0:T(4,128)(2,1)} %reshape.208), calls=%async_computation.3 | async-start | bytes 524288 | tf_op jit(solution)/shard_map/all_to_all | solution.py:191
  364.1 65.6 %collective-permute-start.1 = (bf16[127,512]{1,0:T(8,128)(2,1)}, bf16[127,512]{1,0:T(8,128)(2,1)}, u32[]{:S(2)}, u32[]{:S(2)}) collective-permute-start(bf16[127,512]{1,0:T(8,128)(2,1)} %slice.33), channel_id=1, source_target_pairs={{0,8},{8,16},{16,24},{24,32},{32,40},{40,48},{48,56},{56,64},{64,7... | collective-permute-start | bytes 390152 | tf_op jit(solution)/shard_map/ppermute | solution.py:11
  368.2 29.5 %all-to-all-start.2 = ((bf16[64,4,32]{2,1,0:T(4,128)(2,1)}), bf16[64,4,32]{2,1,0:T(4,128)(2,1)S(1)}, u32[]{:S(2)}, u32[]{:S(2)}) async-start(bf16[64,4,32]{2,1,0:T(4,128)(2,1)} %bitcast.49), calls=%async_computation.2 | async-start | bytes 131072 | tf_op jit(solution)/shard_map/all_to_all | solution.py:190
  397.7 30.3 %all-to-all-start = ((bf16[64,4,32]{2,1,0:T(4,128)(2,1)}), bf16[64,4,32]{2,1,0:T(4,128)(2,1)S(1)}, u32[]{:S(2)}, u32[]{:S(2)}) async-start(bf16[64,4,32]{2,1,0:T(4,128)(2,1)} %bitcast.46), calls=%async_computation | async-start | bytes 131072 | tf_op jit(solution)/shard_map/all_to_all | solution.py:192
  431.8 7.9 %copy-start.6 = (f32[32]{0:T(128)S(1)}, f32[32]{0:T(128)}, u32[]{:S(2)}) copy-start(f32[32]{0:T(128)} %copy-done.5) | copy-start | bytes 388
Sparse Core Ops, SparseCore 0:
  11.0 146.2 all-gather.4
  160.2 137.0 all-gather.2
where the time goes:
time: 735 us; the launch traced here: 734 us
  blocking collectives  296 us (40%)
  waiting for transfers between devices  237 us (32%)
  starting transfers between devices  70.3 us (10%)
  local copies, waits for them, and re-layouts  58.2 us (8%)
  matrix products  50 us (7%)
  between operations  14.5 us (2%)
  other arithmetic  7.68 us (1%)
    psum x1, blocking collectives, on_device(): lax.psum((short_tap_grad, medium_tap_grad * decay_envelope), 'seq')  275 us
    all_gather x1, waiting for transfers between devices, on_device(): lax.all_gather(adapter_down_factor, 'seq', axis=0, tiled=True)  136 us
    all_gather x1, waiting for transfers between devices, on_device(): lax.all_gather(adapter_up_factor, 'seq', axis=0, tiled=True)  83.2 us
    dot_general x24, matrix products, one_block(): jnp.einsum('gts,gcs->gct', band, data, precision=lax.Precision.HIGHEST)  28.5 us
    reshape x24, local copies, waits for them, and re-layouts, band_matrix(): return repeated_groups.reshape(groups, out_len, full_len)  25.7 us
    psum x1, blocking collectives, on_device(): lax.psum(select_codes(contract_last(normalized_layer_entry, flat_down), o...  20.7 us
    all_to_all x1, starting transfers between devices, on_device(): lax.all_to_all(packed[0], 'seq', split_axis=0, concat_axis=0, tiled=True)  20.2 us
    all_to_all x1, starting transfers between devices, on_device(): lax.all_to_all(packed[3], 'seq', split_axis=0, concat_axis=0, tiled=True)  15.4 us
  transfers between devices with their start and end apart: 10, of which 4 were waited for; matrix products, arithmetic and copies ran while one was open for 13% of the time, Pallas kernels for 0%

commit v1 on v0

--- a/solution.py
+++ b/solution.py
@@ -113,9 +113,16 @@
     owner_hot = (owner_token[:, None] == jnp.arange(seq_count, dtype=jnp.float32)[None, :]).astype(
         jnp.float32
     )
+
+    def cut_lots_all(local_x):
+        all_values = jnp.concatenate(
+            lax.all_to_all(jnp.stack([local_x] * lax.psum(1, "seq")), "seq", 0, 0), axis=0
+        )
+        return all_values
+
     all_down, all_up = (
         lax.all_gather(adapter_down_factor, "seq", axis=0, tiled=True),
-        lax.all_gather(adapter_up_factor, "seq", axis=0, tiled=True),
+        cut_lots_all(adapter_up_factor),
     )
     flat_down = all_down.reshape(seq_count * lowdim_breadth, feature_lanes)
     flat_up = all_up.reshape(seq_count * lowdim_breadth, feature_lanes)

time: 735 us -> 639 us (0.87)
  waiting for transfers between devices: 237 us -> 126 us
  starting transfers between devices: 70.3 us -> 83.1 us
    all_gather x1 -> x0, waiting for transfers between devices: 83.2 us -> none  [on_device(): lax.all_gather(adapter_up_factor, 'seq', axis=0, tiled=True)]
    all_gather x1, waiting for transfers between devices: 136 us -> 106 us  [on_device(): lax.all_gather(adapter_down_factor, 'seq', axis=0, tiled=True)]
    all_to_all x0 -> x1, starting transfers between devices: none -> 19.1 us  [cut_lots_all(): lax.all_to_all(jnp.stack([local_x] * lax.psum(1, 'seq')), 'seq', 0, 0)]
    all_to_all x1, starting transfers between devices: 20.2 us -> 10.2 us  [on_device(): lax.all_to_all(packed[0], 'seq', split_axis=0, concat_axis=0, tiled=True)]
  transfers between devices with their start and end apart: 10 -> 10, of which waited for: 4 -> 4; matrix products, arithmetic and copies ran while one was open for 13% -> 14% of each run, Pallas kernels for 0% -> 0%
where the time goes in v1:
time: 639 us; the launch traced here: 638 us
  blocking collectives  296 us (46%)
  waiting for transfers between devices  126 us (20%)
  starting transfers between devices  83.1 us (13%)
  local copies, waits for them, and re-layouts  60.6 us (9%)
  matrix products  49.9 us (8%)
  between operations  14.6 us (2%)
  other arithmetic  6.51 us (1%)
    psum x1, blocking collectives, on_device(): lax.psum((short_tap_grad, medium_tap_grad * decay_envelope), 'seq')  275 us
    all_gather x1, waiting for transfers between devices, on_device(): lax.all_gather(adapter_down_factor, 'seq', axis=0, tiled=True)  106 us
    dot_general x24, matrix products, one_block(): jnp.einsum('gts,gcs->gct', band, data, precision=lax.Precision.HIGHEST)  31 us
    reshape x24, local copies, waits for them, and re-layouts, band_matrix(): return repeated_groups.reshape(groups, out_len, full_len)  25.7 us
    psum x1, blocking collectives, on_device(): lax.psum(select_codes(contract_last(normalized_layer_entry, flat_down), o...  21.3 us
    all_to_all x1, starting transfers between devices, cut_lots_all(): lax.all_to_all(jnp.stack([local_x] * lax.psum(1, 'seq')), 'seq', 0, 0)  19.1 us
    all_to_all x1, starting transfers between devices, on_device(): lax.all_to_all(packed[3], 'seq', split_axis=0, concat_axis=0, tiled=True)  14.9 us
    all_to_all x1, starting transfers between devices, on_device(): lax.all_to_all(packed[2], 'seq', split_axis=0, concat_axis=0, tiled=True)  14.7 us
  transfers between devices with their start and end apart: 10, of which 4 were waited for; matrix products, arithmetic and copies ran while one was open for 14% of the time, Pallas kernels for 0%

profile of v1, /device:TPU:2, one launch (start us, length us, event | category | flops | bytes accessed | tf_op | source)
XLA Modules:
  0.0 638.5 jit_solution(3855336073341729385)
XLA Ops:
  7.2 2.4 stack.2
  9.6 19.1 %all-to-all-start = ((bf16[64,1,32,512]{3,2,1,0:T(8,128)(2,1)}), bf16[64,1,32,512]{3,2,1,0:T(8,128)(2,1)}, u32[]{:S(2)}, u32[]{:S(2)}) async-start(bf16[64,1,32,512]{3,2,1,0:T(8,128)(2,1)} %stack.2), calls=%async_computation | async-start | bytes 4194304 | tf_op jit(solution)/shard_map/all_to_all | solution.py:119
  31.9 4.7 collective-permute-done.2
  38.4 12.9 %while.70 = (s32[]{:T(128)}, f32[4,8,16,128]{3,2,1,0:T(8,128)}, f32[4,8,16,255]{3,2,1,0:T(8,128)S(1)}, f32[4,8,128]{2,1,0:T(8,128)S(1)}, s32[]{:T(128)}, /*index=5*/f32[]{:T(128)}) while((s32[]{:T(128)}, f32[4,8,16,128]{3,2,1,0:T(8,128)}, f32[4,8,16,255]{3,2,1,0:T(8,128)S(1)}, f32[4,8,128]{2,1,0:T(8,128)S(1)}, s32[]{:T(128)}, ...), condition=%wide.region_8.9_spmd, body=%wide.region_7.8_spmd.sunk | while | flops 50135040 | bytes 6509645 | solution.py:40
  56.5 2.7 collective-permute-done.3
  60.7 14.3 %while.71 = (s32[]{:T(128)}, f32[4,8,16,128]{3,2,1,0:T(8,128)}, f32[4,8,16,134]{3,2,1,0:T(8,128)S(1)}, f32[4,8,7]{2,1,0:T(8,128)S(1)}, s32[]{:T(128)}, /*index=5*/f32[]{:T(128)}) while((s32[]{:T(128)}, f32[4,8,16,128]{3,2,1,0:T(8,128)}, f32[4,8,16,134]{3,2,1,0:T(8,128)S(1)}, f32[4,8,7]{2,1,0:T(8,128)S(1)}, s32[]{:T(128)}, ...), condition=%wide.region_10.11_spmd, body=%wide.region_9.10_spmd.sunk | while | flops 26345472 | bytes 5110381 | solution.py:40
  78.1 105.7 %all-gather.2.cloned.1.call-done = bf16[64,32,512]{2,1,0:T(8,128)(2,1)} async-done(((bf16[1,32,512]{2,1,0:T(8,128)(2,1)}), bf16[64,32,512]{2,1,0:T(8,128)(2,1)}) %all-gather.2.cloned.1.call-update) | async-done | bytes 2097168 | tf_op jit(solution)/shard_map/all_gather | solution.py:124
  183.8 4.0 fusion.44
  187.8 10.2 %all-to-all-start.2 = ((bf16[64,4,512]{2,1,0:T(4,128)(2,1)}), bf16[64,4,512]{2,1,0:T(4,128)(2,1)S(1)}, u32[]{:S(2)}, u32[]{:S(2)}) async-start(bf16[64,4,512]{2,1,0:T(4,128)(2,1)} %reshape.216), calls=%async_computation.2 | async-start | bytes 524288 | tf_op jit(solution)/shard_map/all_to_all | solution.py:196
  198.1 4.1 fusion.41
  202.1 21.3 %all-reduce.7 = (bf16[128,32]{0,1:T(8,128)(2,1)S(1)}, bf16[128,32]{0,1:T(8,128)(2,1)S(1)}) all-reduce(f32[128,32]{0,1:T(8,128)S(1)} %fusion.44, f32[128,32]{0,1:T(8,128)S(1)} %fusion.41), channel_id=1, replica_groups=mesh['seq'=64,'ch'=8] {'ch'}, use_global_device_ids=true, to_apply=%region_2.0 | all-reduce | flops 8192 | bytes 49152 | tf_op jit(solution)/shard_map/psum | solution.py:129
  224.0 2.3 fusion.57
  226.3 3.3 collective-permute-start
  229.8 3.1 fusion.54
  235.0 14.7 %all-to-all-start.4 = ((bf16[64,4,512]{2,1,0:T(4,128)(2,1)}), bf16[64,4,512]{2,1,0:T(4,128)(2,1)}, u32[]{:S(2)}, u32[]{:S(2)}) async-start(bf16[64,4,512]{2,1,0:T(4,128)(2,1)} %reshape.219), calls=%async_computation.4 | async-start | bytes 524288 | tf_op jit(solution)/shard_map/all_to_all | solution.py:198
  250.4 14.3 %while.68 = (s32[]{:T(128)}, f32[4,8,16,128]{3,2,1,0:T(8,128)}, f32[4,8,16,134]{3,2,1,0:T(8,128)S(1)}, f32[4,8,7]{2,1,0:T(8,128)S(1)}, s32[]{:T(128)}, /*index=5*/f32[]{:T(128)}) while((s32[]{:T(128)}, f32[4,8,16,128]{3,2,1,0:T(8,128)}, f32[4,8,16,134]{3,2,1,0:T(8,128)S(1)}, f32[4,8,7]{2,1,0:T(8,128)S(1)}, s32[]{:T(128)}, ...), condition=%wide.region_4.5_spmd, body=%wide.region_3.0_spmd.sunk | while | flops 26345472 | bytes 5110381 | solution.py:40
  268.3 4.1 collective-permute-start.1
  272.3 14.3 %all-to-all-start.3 = ((bf16[64,4,32]{2,1,0:T(4,128)(2,1)}), bf16[64,4,32]{2,1,0:T(4,128)(2,1)S(1)}, u32[]{:S(2)}, u32[]{:S(2)}) async-start(bf16[64,4,32]{2,1,0:T(4,128)(2,1)} %bitcast.52), calls=%async_computation.3 | async-start | bytes 131072 | tf_op jit(solution)/shard_map/all_to_all | solution.py:197
  287.2 14.1 %while.72 = (s32[]{:T(128)}, f32[4,8,7]{2,1,0:T(8,128)}, f32[4,8,16,128]{3,2,1,0:T(8,128)S(1)}, f32[4,8,16,134]{3,2,1,0:T(8,128)S(1)}, s32[]{:T(128)}, /*index=5*/s32[]{:T(128)}, f32[]{:T(128)}) while((s32[]{:T(128)}, f32[4,8,7]{2,1,0:T(8,128)}, f32[4,8,16,128]{3,2,1,0:T(8,128)S(1)}, f32[4,8,16,134]{3,2,1,0:T(8,128)S(1)}, s32[]{:T(128)}, ...), condition=%wide.region_16.17_spmd, body=%wide.region_14.16_spmd.sunk | while | flops 26482636 | bytes 4614565 | solution.py:40
  302.1 14.9 %all-to-all-start.1 = ((bf16[64,4,32]{2,1,0:T(4,128)(2,1)}), bf16[64,4,32]{2,1,0:T(4,128)(2,1)S(1)}, u32[]{:S(2)}, u32[]{:S(2)}) async-start(bf16[64,4,32]{2,1,0:T(4,128)(2,1)} %bitcast.49), calls=%async_computation.1 | async-start | bytes 131072 | tf_op jit(solution)/shard_map/all_to_all | solution.py:199
  318.7 13.4 %all-to-all-done.1 = bf16[64,4,32]{2,1,0:T(4,128)(2,1)S(1)} async-done(((bf16[64,4,32]{2,1,0:T(4,128)(2,1)}), bf16[64,4,32]{2,1,0:T(4,128)(2,1)S(1)}, u32[]{:S(2)}, u32[]{:S(2)}) %all-to-all-start.1) | async-done | bytes 16416 | tf_op jit(solution)/shard_map/all_to_all | solution.py:199
  336.0 7.9 %while.73 = (s32[]{:T(128)}, f32[4,8,128]{2,1,0:T(8,128)S(1)}, f32[4,8,16,128]{3,2,1,0:T(8,128)S(1)}, f32[4,8,16,255]{3,2,1,0:T(8,128)S(1)}, s32[]{:T(128)}, /*index=5*/s32[]{:T(128)}, f32[]{:T(128)}) while((s32[]{:T(128)}, f32[4,8,128]{2,1,0:T(8,128)S(1)}, f32[4,8,16,128]{3,2,1,0:T(8,128)S(1)}, f32[4,8,16,255]{3,2,1,0:T(8,128)S(1)}, ...), condition=%wide.region_20.21_spmd, body=%wide.region_18.20_spmd.sunk | while | flops 50395136 | bytes 6505573 | solution.py:40
  344.0 275.1 %all-reduce.6 = (f32[32,7]{0,1:T(8,128)S(1)}, f32[32,128]{1,0:T(8,128)S(1)}) all-reduce(f32[32,7]{0,1:T(8,128)S(1)} %copy.96, f32[32,128]{1,0:T(8,128)S(1)} %bitcast_multiply_fusion), channel_id=1, replica_groups=mesh['seq'=64,'ch'=8] {'seq'}, use_global_device_ids=true, to_apply=%region_17.18 | all-reduce | flops 4320 | bytes 34560 | tf_op jit(solution)/shard_map/psum | solution.py:173
  620.3 10.5 %while.69 = (s32[]{:T(128)}, f32[4,8,16,128]{3,2,1,0:T(8,128)S(1)}, f32[4,8,16,255]{3,2,1,0:T(8,128)S(1)}, f32[4,8,128]{2,1,0:T(8,128)S(1)}, s32[]{:T(128)}, /*index=5*/f32[]{:T(128)}) while((s32[]{:T(128)}, f32[4,8,16,128]{3,2,1,0:T(8,128)S(1)}, f32[4,8,16,255]{3,2,1,0:T(8,128)S(1)}, f32[4,8,128]{2,1,0:T(8,128)S(1)}, s32[]{:T(128)}, ...), condition=%wide.region_6.7_spmd, body=%wide.region_5.6_spmd.sunk | while | flops 50135040 | bytes 6509645 | solution.py:40
  (287 shorter events, 103.8 us)
Async XLA Ops:
  7.2 23.6 %copy-start = (bf16[128,512]{1,0:T(8,128)(2,1)S(1)}, bf16[128,512]{1,0:T(8,128)(2,1)}, u32[]{:S(2)}) copy-start(bf16[128,512]{1,0:T(8,128)(2,1)} %param.26) | copy-start | bytes 393220
  9.6 19.2 %copy-start.5 = (bf16[128,512]{1,0:T(8,128)(2,1)S(1)}, bf16[128,512]{1,0:T(8,128)(2,1)}, u32[]{:S(2)}) copy-start(bf16[128,512]{1,0:T(8,128)(2,1)} %param.30) | copy-start | bytes 393220
  9.6 19.4 %copy-start.6 = (bf16[128,512]{1,0:T(8,128)(2,1)S(1)}, bf16[128,512]{1,0:T(8,128)(2,1)}, u32[]{:S(2)}) copy-start(bf16[128,512]{1,0:T(8,128)(2,1)} %param.32) | copy-start | bytes 393220
  9.6 20.9 %copy-start.15 = (s32[64]{0:T(128)S(1)}, s32[64]{0:T(128)}, u32[]{:S(2)}) copy-start(s32[64]{0:T(128)} %param.36) | copy-start | bytes 772
  9.6 20.9 %copy-start.16 = (s32[128,1]{0,1:T(1,128)S(1)}, s32[128,1]{0,1:T(1,128)}, u32[]{:S(2)}) copy-start(s32[128,1]{0,1:T(1,128)} %param.35) | copy-start | bytes 1540
  9.6 21.7 %copy-start.17 = (f32[32]{0:T(128)S(1)}, f32[32]{0:T(128)}, u32[]{:S(2)}) copy-start(f32[32]{0:T(128)} %param.39) | copy-start | bytes 388
  9.6 21.7 %copy-start.7 = (f32[32,128]{1,0:T(8,128)S(1)}, f32[32,128]{1,0:T(8,128)}, u32[]{:S(2)}) copy-start(f32[32,128]{1,0:T(8,128)} %param.38) | copy-start | bytes 49156
  9.6 178.2 %all-to-all-start = ((bf16[64,1,32,512]{3,2,1,0:T(8,128)(2,1)}), bf16[64,1,32,512]{3,2,1,0:T(8,128)(2,1)}, u32[]{:S(2)}, u32[]{:S(2)}) async-start(bf16[64,1,32,512]{3,2,1,0:T(8,128)(2,1)} %stack.2), calls=%async_computation | async-start | bytes 4194304 | tf_op jit(solution)/shard_map/all_to_all | solution.py:119
  28.8 155.0 %all-gather.2.cloned.1.call-start = ((), (), s32[]{:S(2)}) async-start(), calls=%async_computation.5 | async-start | bytes 2129920 | tf_op jit(solution)/shard_map/all_gather | solution.py:124
  29.1 7.5 %collective-permute-start.2 = (bf16[127,512]{0,1:T(8,128)(2,1)S(1)}, bf16[127,512]{0,1:T(8,128)(2,1)S(1)}, u32[]{:S(2)}, u32[]{:S(2)}) collective-permute-start(bf16[127,512]{0,1:T(8,128)(2,1)S(1)} %bitcast.203), channel_id=1, source_target_pairs={{8,0},{16,8},{24,16},{32,24},{40,32},{48,40},{56,48},{64,56},{72,6... | collective-permute-start | bytes 390152 | tf_op jit(solution)/shard_map/ppermute | solution.py:11
  38.4 14.1 %copy-start.2 = (bf16[128,512]{1,0:T(8,128)(2,1)S(1)}, bf16[128,512]{1,0:T(8,128)(2,1)}, u32[]{:S(2)}) copy-start(bf16[128,512]{1,0:T(8,128)(2,1)} %param.27) | copy-start | bytes 393220
  38.4 17.1 %copy-start.8 = (f32[32,7]{0,1:T(8,128)S(1)}, f32[32,7]{0,1:T(8,128)}, u32[]{:S(2)}) copy-start(f32[32,7]{0,1:T(8,128)} %param.37) | copy-start | bytes 2692
  53.5 5.6 collective-permute-start.3
  60.7 15.5 %copy-start.12 = (f32[128]{0:T(128)S(1)}, f32[128]{0:T(128)}, u32[]{:S(2)}) copy-start(f32[128]{0:T(128)} %copy-done.11) | copy-start | bytes 1540
  77.4 120.7 %copy-start.3 = (bf16[128,512]{1,0:T(8,128)(2,1)S(1)}, bf16[128,512]{1,0:T(8,128)(2,1)}, u32[]{:S(2)}) copy-start(bf16[128,512]{1,0:T(8,128)(2,1)} %param.28) | copy-start | bytes 393220
  187.8 47.2 %all-to-all-start.2 = ((bf16[64,4,512]{2,1,0:T(4,128)(2,1)}), bf16[64,4,512]{2,1,0:T(4,128)(2,1)S(1)}, u32[]{:S(2)}, u32[]{:S(2)}) async-start(bf16[64,4,512]{2,1,0:T(4,128)(2,1)} %reshape.216), calls=%async_computation.2 | async-start | bytes 524288 | tf_op jit(solution)/shard_map/all_to_all | solution.py:196
  198.0 25.9 %copy-start.4 = (bf16[128,512]{1,0:T(8,128)(2,1)S(1)}, bf16[128,512]{1,0:T(8,128)(2,1)}, u32[]{:S(2)}) copy-start(bf16[128,512]{1,0:T(8,128)(2,1)} %param.29) | copy-start | bytes 393220
  226.3 8.4 %collective-permute-start = (bf16[6,512]{1,0:T(8,128)(2,1)S(1)}, bf16[6,512]{1,0:T(8,128)(2,1)S(1)}, u32[]{:S(2)}, u32[]{:S(2)}) collective-permute-start(bf16[6,512]{1,0:T(8,128)(2,1)S(1)} %slice.32), channel_id=1, source_target_pairs={{0,8},{8,16},{16,24},{24,32},{32,40},{40,48},{48,56},{56,64},{64,7... | collective-permute-start | bytes 18440 | tf_op jit(solution)/shard_map/ppermute | solution.py:11
  235.0 15.4 %copy-start.1 = (bf16[64,4,512]{2,1,0:T(4,128)(2,1)}, bf16[64,4,512]{2,1,0:T(4,128)(2,1)S(1)}, u32[]{:S(2)}) copy-start(bf16[64,4,512]{2,1,0:T(4,128)(2,1)S(1)} %all-to-all-done.2) | copy-start | bytes 786436
  235.0 37.3 %all-to-all-start.4 = ((bf16[64,4,512]{2,1,0:T(4,128)(2,1)}), bf16[64,4,512]{2,1,0:T(4,128)(2,1)}, u32[]{:S(2)}, u32[]{:S(2)}) async-start(bf16[64,4,512]{2,1,0:T(4,128)(2,1)} %reshape.219), calls=%async_computation.4 | async-start | bytes 524288 | tf_op jit(solution)/shard_map/all_to_all | solution.py:198
  268.3 65.6 %collective-permute-start.1 = (bf16[127,512]{1,0:T(8,128)(2,1)}, bf16[127,512]{1,0:T(8,128)(2,1)}, u32[]{:S(2)}, u32[]{:S(2)}) collective-permute-start(bf16[127,512]{1,0:T(8,128)(2,1)} %slice.33), channel_id=1, source_target_pairs={{0,8},{8,16},{16,24},{24,32},{32,40},{40,48},{48,56},{56,64},{64,7... | collective-permute-start | bytes 390152 | tf_op jit(solution)/shard_map/ppermute | solution.py:11
  272.3 29.8 %all-to-all-start.3 = ((bf16[64,4,32]{2,1,0:T(4,128)(2,1)}), bf16[64,4,32]{2,1,0:T(4,128)(2,1)S(1)}, u32[]{:S(2)}, u32[]{:S(2)}) async-start(bf16[64,4,32]{2,1,0:T(4,128)(2,1)} %bitcast.52), calls=%async_computation.3 | async-start | bytes 131072 | tf_op jit(solution)/shard_map/all_to_all | solution.py:197
  302.1 30.1 %all-to-all-start.1 = ((bf16[64,4,32]{2,1,0:T(4,128)(2,1)}), bf16[64,4,32]{2,1,0:T(4,128)(2,1)S(1)}, u32[]{:S(2)}, u32[]{:S(2)}) async-start(bf16[64,4,32]{2,1,0:T(4,128)(2,1)} %bitcast.49), calls=%async_computation.1 | async-start | bytes 131072 | tf_op jit(solution)/shard_map/all_to_all | solution.py:199
  336.0 7.9 %copy-start.10 = (f32[32]{0:T(128)S(1)}, f32[32]{0:T(128)}, u32[]{:S(2)}) copy-start(f32[32]{0:T(128)} %copy-done.9) | copy-start | bytes 388
  (4 other events, 7.8 us)
Sparse Core Ops, SparseCore 0:
  32.5 151.2 all-gather.1
